TPU v7x, 32 devices: a whole 2x2x4 slice. The times are simulated.
32 devices in a mesh: patch: 8 (over z, core), visit: 4 (over y, x).
Axes of the slice: x: 2, y: 2, z: 4, core: 2. Of those that a mesh axis runs over, the one named last changes fastest.
Arguments:
- blocks: bfloat16 [8, 4, 16, 256, 256], P('patch', 'visit'), may hold values from -6 to 6
- block_patch: int32 [8, 4, 16, 1], P('patch', 'visit'), may hold values from 0 to 7; in each aligned block of 16 rows (0 to 15, 16 to 31, ..., all dimensions but the last counted through in order) at most 2 rows name the same one
- block_slot: int32 [8, 4, 16], P('patch', 'visit'), may hold values from 0 to 7
- block_count: int32 [8, 4], P('patch', 'visit'), may hold values from 12 to 16, as said below
- template: bfloat16 [8, 512, 1024], P('patch', 'visit'), may hold values from -6 to 6
- basis_rows: bfloat16 [9, 21], replicated, may hold values from -1.25 to 1.25
- basis_cols: float32 [9, 21], replicated, may hold values from -1.25 to 1.25
- coeffs: float32 [4, 9], P('visit'), may hold values from -2 to 2
- psf_rows: bfloat16 [4, 2, 25], P('visit'), may hold values from -1.25 to 1.25
- psf_cols: bfloat16 [4, 2, 25], P('visit'), may hold values from -1.25 to 1.25
Outputs:
- filtered: float32 [8, 4, 512, 1024], P('patch', 'visit')
Inputs may be any that keep to these rules, and one draw needn't show every extreme that they name: `block_patch`: among the 16 entries of one list (one patch index and visit) no patch is named more than 2 times, and some list names a patch exactly 2 times. Entries at positions block_count and beyond are unused.
All inputs are finite; a program needn't handle non-finite values.
Results may differ from a plain program's by a relative error of at most 0.005.
Values may be sent and summed in bfloat16 or wider, within the bound.
A program may use at most 128 MiB of HBM per device.

v0:
```python
import jax
import jax.numpy as jnp
from jax import lax
from jax.sharding import PartitionSpec as P

CAP = 2


def one_hot_bands(length, tile_size):
    band_shape = (3, length, tile_size, tile_size)
    side_ids = lax.broadcasted_iota(jnp.int32, band_shape, 0) - 1
    tap_ids = lax.broadcasted_iota(jnp.int32, band_shape, 1)
    inner = lax.broadcasted_iota(jnp.int32, band_shape, 2)
    outer = lax.broadcasted_iota(jnp.int32, band_shape, 3)
    return (side_ids * tile_size + inner - outer + length // 2 == tap_ids).astype(jnp.float32)


def band_tables(kernel_taps, one_hot):
    return jnp.einsum(
        "cl,dlij->cdij", kernel_taps.astype(jnp.float32), one_hot, precision=lax.Precision.HIGHEST
    ).astype(jnp.bfloat16)


def across_columns(source, tables):
    tile_size = tables.shape[-1]
    height, breadth = source.shape
    tile_count = breadth // tile_size
    tiled = source.reshape(height, tile_count, tile_size)
    zero_block = jnp.zeros((height, 1, tile_size), source.dtype)
    left_side = jnp.concatenate([zero_block, tiled[:, :-1]], axis=1)
    right_side = jnp.concatenate([tiled[:, 1:], zero_block], axis=1)
    summed = jnp.einsum("hbt,ctu->chbu", tiled, tables[:, 1], preferred_element_type=jnp.float32)
    summed = summed + jnp.einsum(
        "hbt,ctu->chbu", left_side, tables[:, 0], preferred_element_type=jnp.float32
    )
    summed = summed + jnp.einsum(
        "hbt,ctu->chbu", right_side, tables[:, 2], preferred_element_type=jnp.float32
    )
    return summed.reshape(tables.shape[0], height, breadth)


def across_rows(source, tables):
    tile_size = tables.shape[-1]
    channels, height, breadth = source.shape
    tile_count = height // tile_size
    tiled = source.reshape(channels, tile_count, tile_size, breadth)
    zero_block = jnp.zeros((channels, 1, tile_size, breadth), source.dtype)
    left_side = jnp.concatenate([zero_block, tiled[:, :-1]], axis=1)
    right_side = jnp.concatenate([tiled[:, 1:], zero_block], axis=1)
    summed = jnp.einsum("cbin,cij->bjn", tiled, tables[:, 1], preferred_element_type=jnp.float32)
    summed = summed + jnp.einsum(
        "cbin,cij->bjn", left_side, tables[:, 0], preferred_element_type=jnp.float32
    )
    summed = summed + jnp.einsum(
        "cbin,cij->bjn", right_side, tables[:, 2], preferred_element_type=jnp.float32
    )
    return summed.reshape(height, breadth)


def place_blocks(
    blocks, block_patch, block_slot, block_count, capacity, slot_total, height, breadth
):
    count_here = blocks.shape[2]
    block_edge = blocks.shape[3]
    pieces = blocks.reshape(count_here, block_edge * block_edge)
    destination = block_patch.reshape(count_here)
    slot_index = block_slot.reshape(count_here)
    row_order = lax.broadcasted_iota(jnp.int32, (count_here, count_here), 0)
    col_order = lax.broadcasted_iota(jnp.int32, (count_here, count_here), 1)
    same_patch = destination[:, None] == destination[None, :]
    earlier = jnp.sum((same_patch & (col_order < row_order)).astype(jnp.int32), axis=1)
    target = destination * capacity + earlier
    live_mask = lax.iota(jnp.int32, count_here) < block_count.reshape(())
    n_patch = lax.axis_size("patch")
    places = n_patch * capacity
    place_ids = lax.broadcasted_iota(jnp.int32, (places, count_here), 0)
    picker = ((place_ids == target[None, :]) & live_mask[None, :]).astype(jnp.float32)
    outgoing = jnp.dot(
        picker.astype(jnp.bfloat16), pieces, preferred_element_type=jnp.float32
    ).astype(jnp.bfloat16)
    outgoing = outgoing.reshape(n_patch, capacity, block_edge * block_edge)
    labels = (
        jnp.dot(
            picker, (slot_index - slot_total).astype(jnp.float32), precision=lax.Precision.HIGHEST
        )
        + slot_total
    )
    labels = labels.astype(jnp.bfloat16).reshape(n_patch, capacity)
    arrived, arrived_slots = (
        lax.all_to_all(outgoing, "patch", split_axis=0, concat_axis=0, tiled=True),
        lax.all_to_all(labels, "patch", split_axis=0, concat_axis=0, tiled=True),
    )
    arrived = arrived.reshape(places, block_edge * block_edge)
    slot_ids = lax.broadcasted_iota(jnp.float32, (slot_total, places), 0)
    chosen = (slot_ids == arrived_slots.reshape(1, places).astype(jnp.float32)).astype(jnp.bfloat16)
    placed = jnp.dot(chosen, arrived, preferred_element_type=jnp.float32)
    tall_count = height // block_edge
    wide_count = breadth // block_edge
    placed = placed.reshape(tall_count, wide_count, block_edge, block_edge).transpose(0, 2, 1, 3)
    return placed.reshape(height, breadth)


def per_device(
    blocks,
    block_patch,
    block_slot,
    block_count,
    template,
    basis_rows,
    basis_cols,
    coeffs,
    psf_rows,
    psf_cols,
):
    local_rows = template.shape[1]
    breadth = template.shape[2]
    height = local_rows * lax.axis_size("visit")
    block_edge = blocks.shape[3]
    slot_total = height // block_edge * (breadth // block_edge)
    science = place_blocks(
        blocks, block_patch, block_slot, block_count, CAP, slot_total, height, breadth
    )
    column_hot = one_hot_bands(basis_rows.shape[1], min(128, breadth))
    row_hot = one_hot_bands(basis_cols.shape[1], min(128, height))
    scaled = (coeffs[0][:, None] * basis_cols).astype(jnp.bfloat16)
    start_image = jnp.zeros((height, breadth), jnp.float32)
    all_tables = band_tables(basis_rows, column_hot)
    partial_rows = across_columns(template[0], all_tables).astype(jnp.bfloat16)
    smoothed_all = lax.all_gather(partial_rows, "visit", axis=1, tiled=True)

    def per_stack(model_image, profiles):
        smoothed, col_taps = profiles
        col_table = band_tables(col_taps[None], row_hot)
        return (model_image + across_rows(smoothed[None], col_table), None)

    model_image = lax.scan(per_stack, start_image, (smoothed_all, scaled))[0]
    difference = (science - model_image).astype(jnp.bfloat16)
    psf_column_hot = one_hot_bands(psf_rows.shape[2], min(128, breadth))
    psf_row_hot = one_hot_bands(psf_cols.shape[2], min(128, height))
    blurred = across_columns(difference, band_tables(psf_rows[0], psf_column_hot)).astype(
        jnp.bfloat16
    )
    filtered = across_rows(blurred, band_tables(psf_cols[0], psf_row_hot))
    return filtered[None, None]


def solution(mesh):
    placed = (
        P("patch", "visit", None, None, None),
        P("patch", "visit", None, None),
        P("patch", "visit", None),
        P("patch", "visit"),
        P("patch", "visit", None),
        P(),
        P(),
        P("visit", None),
        P("visit", None, None),
        P("visit", None, None),
    )
    return jax.shard_map(
        per_device,
        mesh=mesh,
        in_specs=placed,
        out_specs=P("patch", "visit", None, None),
        check_vma=False,
    )
```

profile of v0, /device:TPU:0, one launch (start us, length us, event | category | flops | bytes accessed | tf_op | source)
XLA Modules:
  0.0 238.5 jit_solution(14624126274584516626)
XLA Ops:
  12.6 2.4 %copy.80 = bf16[9,128,1024]{2,1,0:T(8,128)(2,1)} copy(bf16[9,128,1024]{1,2,0:T(8,128)(2,1)S(1)} %bitcast.214) | data formatting | bytes 4718592 | tf_op jit(solution)/shard_map/convert_element_type | solution.py:128
  16.9 6.4 %all-to-all-start = ((bf16[8,1,2]{2,1,0:T(2,128)(2,1)}), bf16[8,1,2]{2,1,0:T(2,128)(2,1)S(1)}, u32[]{:S(2)}, u32[]{:S(2)}) async-start(bf16[8,1,2]{2,1,0:T(2,128)(2,1)} %all_to_all.12), calls=%async_computation | async-start | bytes 8192 | tf_op jit(solution)/shard_map/all_to_all | solution.py:91
  25.1 2.3 reshape.116
  28.8 4.5 %all-to-all-start.1 = ((bf16[8,2,65536]{2,1,0:T(2,128)(2,1)}), bf16[8,2,65536]{2,1,0:T(2,128)(2,1)}, u32[]{:S(2)}, u32[]{:S(2)}) async-start(bf16[8,2,65536]{2,1,0:T(2,128)(2,1)} %reshape.116), calls=%async_computation.1 | async-start | bytes 4194304 | tf_op jit(solution)/shard_map/all_to_all | solution.py:90
  37.3 44.9 %all-to-all-done.1 = bf16[8,2,65536]{2,1,0:T(2,128)(2,1)} async-done(((bf16[8,2,65536]{2,1,0:T(2,128)(2,1)}), bf16[8,2,65536]{2,1,0:T(2,128)(2,1)}, u32[]{:S(2)}, u32[]{:S(2)}) %all-to-all-start.1) | async-done | bytes 2097184 | tf_op jit(solution)/shard_map/all_to_all | solution.py:90
  82.2 2.1 reshape.117
  85.3 1.8 copy.81
  87.1 27.0 %all-gather.2.cloned.1.call-done = bf16[9,512,1024]{2,1,0:T(8,128)(2,1)} async-done(((bf16[9,128,1024]{2,1,0:T(8,128)(2,1)}), bf16[9,512,1024]{2,1,0:T(8,128)(2,1)}) %all-gather.2.cloned.1.call-update) | async-done | bytes 9437200 | tf_op jit(solution)/shard_map/all_gather | solution.py:129
  114.1 97.7 %while.11 = (s32[]{:T(128)}, f32[512,1024]{1,0:T(8,128)}, bf16[9,21]{1,0:T(8,128)(2,1)S(1)}, bf16[9,512,1024]{2,1,0:T(8,128)(2,1)}, s32[3]{0:T(128)S(1)}, /*index=5*/s32[]{:T(128)}, s32[]{:T(128)}) while((s32[]{:T(128)}, f32[512,1024]{1,0:T(8,128)}, bf16[9,21]{1,0:T(8,128)(2,1)S(1)}, bf16[9,512,1024]{2,1,0:T(8,128)(2,1)}, ...), condition=%wide.region_2.3_spmd.clone, body=%wide.region_1.2_spmd.clone.sunk | while | flops 422297600 | bytes 33489512 | solution.py:136
  114.7 4.0 %fusion.117 = bf16[1,3,128,128]{3,0,2,1:T(2,128)(2,1)S(1)} fusion(f32[3,21,128,128]{3,2,1,0:T(8,128)S(1)} %fusion.116, bf16[9,21]{1,0:T(8,128)(2,1)S(1)} %get-tuple-element.132, s32[]{:T(128)} %get-tuple-element.123), kind=kOutput, calls=%fused_computation.1.clone.1 | convolution fusion | flops 12386304 | bytes 4227588 | tf_op jit(solution)/shard_map/while/body/eval_jaxpr/cl,dlij->cdij/dot_general | solution.py:19
  121.6 2.0 bitcast_add_fusion.4
  124.1 4.0 %fusion.117 = bf16[1,3,128,128]{3,0,2,1:T(2,128)(2,1)S(1)} fusion(f32[3,21,128,128]{3,2,1,0:T(8,128)S(1)} %fusion.116, bf16[9,21]{1,0:T(8,128)(2,1)S(1)} %get-tuple-element.132, s32[]{:T(128)} %get-tuple-element.123), kind=kOutput, calls=%fused_computation.1.clone.1 | convolution fusion | flops 12386304 | bytes 4227588 | tf_op jit(solution)/shard_map/while/body/eval_jaxpr/cl,dlij->cdij/dot_general | solution.py:19
  131.0 3.6 %bitcast_add_fusion.4 = f32[512,1024]{1,0:T(8,128)} fusion(f32[128,4,1024]{2,0,1:T(8,128)S(1)} %add_add_fusion.2, f32[512,1024]{1,0:T(8,128)} %get-tuple-element.124, pred[]{:T(512)S(6)} %compare.11), kind=kLoop, calls=%fused_computation.5.clone.1 | loop fusion | flops 1048576 | bytes 6291457 | tf_op jit(solution)/shard_map/while/body/eval_jaxpr/add | solution.py:134
  135.2 4.0 %fusion.117 = bf16[1,3,128,128]{3,0,2,1:T(2,128)(2,1)S(1)} fusion(f32[3,21,128,128]{3,2,1,0:T(8,128)S(1)} %fusion.116, bf16[9,21]{1,0:T(8,128)(2,1)S(1)} %get-tuple-element.132, s32[]{:T(128)} %get-tuple-element.123), kind=kOutput, calls=%fused_computation.1.clone.1 | convolution fusion | flops 12386304 | bytes 4227588 | tf_op jit(solution)/shard_map/while/body/eval_jaxpr/cl,dlij->cdij/dot_general | solution.py:19
  142.0 3.6 %bitcast_add_fusion.4 = f32[512,1024]{1,0:T(8,128)} fusion(f32[128,4,1024]{2,0,1:T(8,128)S(1)} %add_add_fusion.2, f32[512,1024]{1,0:T(8,128)} %get-tuple-element.124, pred[]{:T(512)S(6)} %compare.11), kind=kLoop, calls=%fused_computation.5.clone.1 | loop fusion | flops 1048576 | bytes 6291457 | tf_op jit(solution)/shard_map/while/body/eval_jaxpr/add | solution.py:134
  146.2 4.0 %fusion.117 = bf16[1,3,128,128]{3,0,2,1:T(2,128)(2,1)S(1)} fusion(f32[3,21,128,128]{3,2,1,0:T(8,128)S(1)} %fusion.116, bf16[9,21]{1,0:T(8,128)(2,1)S(1)} %get-tuple-element.132, s32[]{:T(128)} %get-tuple-element.123), kind=kOutput, calls=%fused_computation.1.clone.1 | convolution fusion | flops 12386304 | bytes 4227588 | tf_op jit(solution)/shard_map/while/body/eval_jaxpr/cl,dlij->cdij/dot_general | solution.py:19
  153.1 3.6 %bitcast_add_fusion.4 = f32[512,1024]{1,0:T(8,128)} fusion(f32[128,4,1024]{2,0,1:T(8,128)S(1)} %add_add_fusion.2, f32[512,1024]{1,0:T(8,128)} %get-tuple-element.124, pred[]{:T(512)S(6)} %compare.11), kind=kLoop, calls=%fused_computation.5.clone.1 | loop fusion | flops 1048576 | bytes 6291457 | tf_op jit(solution)/shard_map/while/body/eval_jaxpr/add | solution.py:134
  157.2 4.0 %fusion.117 = bf16[1,3,128,128]{3,0,2,1:T(2,128)(2,1)S(1)} fusion(f32[3,21,128,128]{3,2,1,0:T(8,128)S(1)} %fusion.116, bf16[9,21]{1,0:T(8,128)(2,1)S(1)} %get-tuple-element.132, s32[]{:T(128)} %get-tuple-element.123), kind=kOutput, calls=%fused_computation.1.clone.1 | convolution fusion | flops 12386304 | bytes 4227588 | tf_op jit(solution)/shard_map/while/body/eval_jaxpr/cl,dlij->cdij/dot_general | solution.py:19
  164.1 3.6 %bitcast_add_fusion.4 = f32[512,1024]{1,0:T(8,128)} fusion(f32[128,4,1024]{2,0,1:T(8,128)S(1)} %add_add_fusion.2, f32[512,1024]{1,0:T(8,128)} %get-tuple-element.124, pred[]{:T(512)S(6)} %compare.11), kind=kLoop, calls=%fused_computation.5.clone.1 | loop fusion | flops 1048576 | bytes 6291457 | tf_op jit(solution)/shard_map/while/body/eval_jaxpr/add | solution.py:134
  168.3 4.0 %fusion.117 = bf16[1,3,128,128]{3,0,2,1:T(2,128)(2,1)S(1)} fusion(f32[3,21,128,128]{3,2,1,0:T(8,128)S(1)} %fusion.116, bf16[9,21]{1,0:T(8,128)(2,1)S(1)} %get-tuple-element.132, s32[]{:T(128)} %get-tuple-element.123), kind=kOutput, calls=%fused_computation.1.clone.1 | convolution fusion | flops 12386304 | bytes 4227588 | tf_op jit(solution)/shard_map/while/body/eval_jaxpr/cl,dlij->cdij/dot_general | solution.py:19
  175.1 3.6 %bitcast_add_fusion.4 = f32[512,1024]{1,0:T(8,128)} fusion(f32[128,4,1024]{2,0,1:T(8,128)S(1)} %add_add_fusion.2, f32[512,1024]{1,0:T(8,128)} %get-tuple-element.124, pred[]{:T(512)S(6)} %compare.11), kind=kLoop, calls=%fused_computation.5.clone.1 | loop fusion | flops 1048576 | bytes 6291457 | tf_op jit(solution)/shard_map/while/body/eval_jaxpr/add | solution.py:134
  179.3 4.0 %fusion.117 = bf16[1,3,128,128]{3,0,2,1:T(2,128)(2,1)S(1)} fusion(f32[3,21,128,128]{3,2,1,0:T(8,128)S(1)} %fusion.116, bf16[9,21]{1,0:T(8,128)(2,1)S(1)} %get-tuple-element.132, s32[]{:T(128)} %get-tuple-element.123), kind=kOutput, calls=%fused_computation.1.clone.1 | convolution fusion | flops 12386304 | bytes 4227588 | tf_op jit(solution)/shard_map/while/body/eval_jaxpr/cl,dlij->cdij/dot_general | solution.py:19
  186.2 3.6 %bitcast_add_fusion.4 = f32[512,1024]{1,0:T(8,128)} fusion(f32[128,4,1024]{2,0,1:T(8,128)S(1)} %add_add_fusion.2, f32[512,1024]{1,0:T(8,128)} %get-tuple-element.124, pred[]{:T(512)S(6)} %compare.11), kind=kLoop, calls=%fused_computation.5.clone.1 | loop fusion | flops 1048576 | bytes 6291457 | tf_op jit(solution)/shard_map/while/body/eval_jaxpr/add | solution.py:134
  190.3 4.0 %fusion.117 = bf16[1,3,128,128]{3,0,2,1:T(2,128)(2,1)S(1)} fusion(f32[3,21,128,128]{3,2,1,0:T(8,128)S(1)} %fusion.116, bf16[9,21]{1,0:T(8,128)(2,1)S(1)} %get-tuple-element.132, s32[]{:T(128)} %get-tuple-element.123), kind=kOutput, calls=%fused_computation.1.clone.1 | convolution fusion | flops 12386304 | bytes 4227588 | tf_op jit(solution)/shard_map/while/body/eval_jaxpr/cl,dlij->cdij/dot_general | solution.py:19
  197.2 3.6 %bitcast_add_fusion.4 = f32[512,1024]{1,0:T(8,128)} fusion(f32[128,4,1024]{2,0,1:T(8,128)S(1)} %add_add_fusion.2, f32[512,1024]{1,0:T(8,128)} %get-tuple-element.124, pred[]{:T(512)S(6)} %compare.11), kind=kLoop, calls=%fused_computation.5.clone.1 | loop fusion | flops 1048576 | bytes 6291457 | tf_op jit(solution)/shard_map/while/body/eval_jaxpr/add | solution.py:134
  201.4 4.0 %fusion.117 = bf16[1,3,128,128]{3,0,2,1:T(2,128)(2,1)S(1)} fusion(f32[3,21,128,128]{3,2,1,0:T(8,128)S(1)} %fusion.116, bf16[9,21]{1,0:T(8,128)(2,1)S(1)} %get-tuple-element.132, s32[]{:T(128)} %get-tuple-element.123), kind=kOutput, calls=%fused_computation.1.clone.1 | convolution fusion | flops 12386304 | bytes 4227588 | tf_op jit(solution)/shard_map/while/body/eval_jaxpr/cl,dlij->cdij/dot_general | solution.py:19
  208.2 3.6 %bitcast_add_fusion.4 = f32[512,1024]{1,0:T(8,128)} fusion(f32[128,4,1024]{2,0,1:T(8,128)S(1)} %add_add_fusion.2, f32[512,1024]{1,0:T(8,128)} %get-tuple-element.124, pred[]{:T(512)S(6)} %compare.11), kind=kLoop, calls=%fused_computation.5.clone.1 | loop fusion | flops 1048576 | bytes 6291457 | tf_op jit(solution)/shard_map/while/body/eval_jaxpr/add | solution.py:134
  211.8 3.0 %copy.82 = f32[512,1024]{0,1:T(8,128)} copy(f32[512,1024]{1,0:T(8,128)} %get-tuple-element.32) | data formatting | bytes 4194304 | tf_op jit(solution)/shard_map/while | solution.py:136
  214.8 2.0 subtract_convert_fusion
  223.4 2.0 convert_element_type.117
  225.5 3.0 %copy.90 = bf16[2,4,128,1024]{3,2,0,1:T(8,128)(2,1)S(1)} copy(bf16[2,4,128,1024]{2,1,3,0:T(4,128)(2,1)} %convert_element_type.117) | data formatting | bytes 4194304 | tf_op jit(solution)/shard_map/convert_element_type | solution.py:140
  229.8 1.9 bitcast_add_fusion.1
  (139 shorter events, 54.0 us)
Async XLA Ops:
  6.5 0.7 copy-start
  6.5 107.6 %all-gather.2.cloned.1.call-start = ((), (), s32[]{:S(2)}) async-start(), calls=%async_computation.2 | async-start | bytes 11796480 | tf_op jit(solution)/shard_map/all_gather | solution.py:129
  8.6 1.0 copy-start.5
  15.0 0.8 copy-start.8
  15.0 1.0 copy-start.9
  15.0 8.2 %copy-start.4 = (bf16[1,1,16,256,256]{4,3,2,1,0:T(8,128)(2,1)S(1)}, bf16[1,1,16,256,256]{4,3,2,1,0:T(8,128)(2,1)}, u32[]{:S(2)}) copy-start(bf16[1,1,16,256,256]{4,3,2,1,0:T(8,128)(2,1)} %param.12) | copy-start | bytes 6291460
  16.9 11.9 %all-to-all-start = ((bf16[8,1,2]{2,1,0:T(2,128)(2,1)}), bf16[8,1,2]{2,1,0:T(2,128)(2,1)S(1)}, u32[]{:S(2)}, u32[]{:S(2)}) async-start(bf16[8,1,2]{2,1,0:T(2,128)(2,1)} %all_to_all.12), calls=%async_computation | async-start | bytes 8192 | tf_op jit(solution)/shard_map/all_to_all | solution.py:91
  27.4 5.9 %copy-start.10 = (bf16[1,2,25]{2,1,0:T(2,128)(2,1)S(1)}, bf16[1,2,25]{2,1,0:T(2,128)(2,1)}, u32[]{:S(2)}) copy-start(bf16[1,2,25]{2,1,0:T(2,128)(2,1)} %param.21) | copy-start | bytes 304
  28.8 53.4 %all-to-all-start.1 = ((bf16[8,2,65536]{2,1,0:T(2,128)(2,1)}), bf16[8,2,65536]{2,1,0:T(2,128)(2,1)}, u32[]{:S(2)}, u32[]{:S(2)}) async-start(bf16[8,2,65536]{2,1,0:T(2,128)(2,1)} %reshape.116), calls=%async_computation.1 | async-start | bytes 4194304 | tf_op jit(solution)/shard_map/all_to_all | solution.py:90
  33.3 2.1 copy-start.6
  33.4 2.1 copy-start.7
  33.4 2.1 copy-start.11
  211.8 3.0 %copy-start.2 = (f32[512,1024]{0,1:T(8,128)S(1)}, f32[512,1024]{0,1:T(8,128)}, u32[]{:S(2)}) copy-start(f32[512,1024]{0,1:T(8,128)} %copy.81) | copy-start | bytes 6291460
  221.5 1.2 copy-start.3
  229.8 1.9 copy-start.1
Sparse Core Ops, SparseCore 0:
  15.1 98.9 all-gather.1
where the time goes:
time: 240 us; the launch traced here: 239 us
  waiting for transfers between devices  73.3 us (31%)
  matrix products  59.7 us (25%)
  local copies, waits for them, and re-layouts  41.5 us (17%)
  other arithmetic  38.2 us (16%)
  between operations  14.5 us (6%)
  starting transfers between devices  10.9 us (5%)
    all_to_all x1, waiting for transfers between devices, place_blocks(): lax.all_to_all(outgoing, 'patch', split_axis=0, concat_axis=0, tiled=True)  44.9 us
    dot_general x12, matrix products, band_tables(): jnp.einsum('cl,dlij->cdij', kernel_taps.astype(jnp.float32), one_hot, pre...  39.9 us
    add x9, other arithmetic, per_stack(): return (model_image + across_rows(smoothed[None], col_table), None)  30.6 us
    all_gather x1, waiting for transfers between devices, per_device(): smoothed_all = lax.all_gather(partial_rows, 'visit', axis=1, tiled=True)  27 us
    dynamic_slice x9, local copies, waits for them, and re-layouts, per_device(): model_image = lax.scan(per_stack, start_image, (smoothed_all, scaled))[0]  11.7 us
    unnamed x31, local copies, waits for them, and re-layouts  6.85 us
    all_to_all x1, starting transfers between devices, place_blocks(): lax.all_to_all(labels, 'patch', split_axis=0, concat_axis=0, tiled=True)  6.35 us
    dot_general x10, matrix products, across_rows(): jnp.einsum('cbin,cij->bjn', left_side, tables[:, 0], preferred_element_ty...  5.32 us
  transfers between devices with their start and end apart: 3, of which 3 were waited for; matrix products, arithmetic and copies ran while one was open for 6% of the time, Pallas kernels for 0%

commit v1 on v0

--- a/solution.py
+++ b/solution.py
@@ -4,6 +4,17 @@
 from jax.sharding import PartitionSpec as P
 
 CAP = 2
+
+
+def fix_rounds_in(w_in, join_dim):
+    axis_id = "visit"
+    chips = lax.axis_size(axis_id)
+    items = [w_in]
+    for no in [*range(chips - 1)]:
+        inter = lax.ppermute(items[-1], axis_id, [(it, (it + 1) % chips) for it in range(chips)])
+        items.append(inter)
+    mixed_arr = jnp.concatenate(items[::-1], axis=join_dim)
+    return jnp.roll(mixed_arr, (lax.axis_index(axis_id) + 1) * w_in.shape[join_dim], axis=join_dim)
 
 
 def one_hot_bands(length, tile_size):
@@ -126,7 +137,7 @@
     start_image = jnp.zeros((height, breadth), jnp.float32)
     all_tables = band_tables(basis_rows, column_hot)
     partial_rows = across_columns(template[0], all_tables).astype(jnp.bfloat16)
-    smoothed_all = lax.all_gather(partial_rows, "visit", axis=1, tiled=True)
+    smoothed_all = fix_rounds_in(partial_rows, 1)
 
     def per_stack(model_image, profiles):
         smoothed, col_taps = profiles

time: 240 us -> 322 us (1.34)
  waiting for transfers between devices: 73.3 us -> 124 us
  local copies, waits for them, and re-layouts: 41.5 us -> 79.9 us
  between operations: 14.5 us -> 0.91 us
  matrix products: 59.7 us -> 64 us
    ppermute x0 -> x3, waiting for transfers between devices: none -> 112 us  [fix_rounds_in(): lax.ppermute(items[-1], axis_id, [(it, (it + 1) % chips) for it in range(...]
    all_to_all x1, waiting for transfers between devices: 44.9 us -> 12.3 us  [place_blocks(): lax.all_to_all(outgoing, 'patch', split_axis=0, concat_axis=0, tiled=True)]
    all_gather x1 -> x0, waiting for transfers between devices: 27 us -> none  [per_device(): smoothed_all = lax.all_gather(partial_rows, 'visit', axis=1, tiled=True)]
    unnamed x31 -> x36, local copies, waits for them, and re-layouts: 6.85 us -> 31.2 us
    dynamic_slice x0 -> x1, local copies, waits for them, and re-layouts: none -> 8.49 us  [fix_rounds_in(): jnp.roll(mixed_arr, (lax.axis_index(axis_id) + 1) * w_in.shape[join_dim],...]
    ppermute x0 -> x3, starting transfers between devices: none -> 3.81 us  [fix_rounds_in(): lax.ppermute(items[-1], axis_id, [(it, (it + 1) % chips) for it in range(...]
  transfers between devices with their start and end apart: 3 -> 5, of which waited for: 3 -> 4; matrix products, arithmetic and copies ran while one was open for 6% -> 7% of each run, Pallas kernels for 0% -> 0%
where the time goes in v1:
time: 322 us; the launch traced here: 321 us
  waiting for transfers between devices  124 us (39%)
  local copies, waits for them, and re-layouts  79.9 us (25%)
  matrix products  64 us (20%)
  other arithmetic  37.4 us (12%)
  starting transfers between devices  13.9 us (4%)
    ppermute x3, waiting for transfers between devices, fix_rounds_in(): lax.ppermute(items[-1], axis_id, [(it, (it + 1) % chips) for it in range(...  112 us
    dot_general x12, matrix products, band_tables(): jnp.einsum('cl,dlij->cdij', kernel_taps.astype(jnp.float32), one_hot, pre...  39.9 us
    unnamed x36, local copies, waits for them, and re-layouts  31.2 us
    add x9, other arithmetic, per_stack(): return (model_image + across_rows(smoothed[None], col_table), None)  29.9 us
    all_to_all x1, waiting for transfers between devices, place_blocks(): lax.all_to_all(outgoing, 'patch', split_axis=0, concat_axis=0, tiled=True)  12.3 us
    dynamic_slice x9, local copies, waits for them, and re-layouts, per_device(): model_image = lax.scan(per_stack, start_image, (smoothed_all, scaled))[0]  11.7 us
    dynamic_slice x1, local copies, waits for them, and re-layouts, fix_rounds_in(): jnp.roll(mixed_arr, (lax.axis_index(axis_id) + 1) * w_in.shape[join_dim],...  8.49 us
  transfers between devices with their start and end apart: 5, of which 4 were waited for; matrix products, arithmetic and copies ran while one was open for 7% of the time, Pallas kernels for 0%

profile of v1, /device:TPU:0, one launch (start us, length us, event | category | flops | bytes accessed | tf_op | source)
XLA Modules:
  0.0 320.6 jit_solution(3079708770498799069)
XLA Ops:
  13.6 52.1 %collective-permute-done = bf16[9,128,1024]{2,1,0:T(8,128)(2,1)} collective-permute-done((bf16[9,128,1024]{2,1,0:T(8,128)(2,1)S(1)}, bf16[9,128,1024]{2,1,0:T(8,128)(2,1)}, u32[]{:S(2)}, u32[]{:S(2)}) %collective-permute-start) | collective-permute-done | bytes 2359328 | tf_op jit(solution)/shard_map/ppermute | solution.py:14
  68.0 4.9 %all-to-all-start = ((bf16[8,1,2]{2,1,0:T(2,128)(2,1)}), bf16[8,1,2]{2,1,0:T(2,128)(2,1)S(1)}, u32[]{:S(2)}, u32[]{:S(2)}) async-start(bf16[8,1,2]{2,1,0:T(2,128)(2,1)} %all_to_all.12), calls=%async_computation | async-start | bytes 8192 | tf_op jit(solution)/shard_map/all_to_all | solution.py:102
  77.7 3.5 %reshape.116 = bf16[8,2,65536]{2,1,0:T(2,128)(2,1)} reshape(bf16[16,65536]{1,0:T(8,128)(2,1)} %convolution_convert_fusion) | data formatting | bytes 4194304 | tf_op jit(solution)/shard_map/reshape | solution.py:92
  81.2 5.2 %all-to-all-start.1 = ((bf16[8,2,65536]{2,1,0:T(2,128)(2,1)}), bf16[8,2,65536]{2,1,0:T(2,128)(2,1)}, u32[]{:S(2)}, u32[]{:S(2)}) async-start(bf16[8,2,65536]{2,1,0:T(2,128)(2,1)} %reshape.116), calls=%async_computation.1 | async-start | bytes 4194304 | tf_op jit(solution)/shard_map/all_to_all | solution.py:101
  86.4 32.9 %collective-permute-done.1 = bf16[9,128,1024]{2,1,0:T(8,128)(2,1)} collective-permute-done((bf16[9,128,1024]{2,1,0:T(8,128)(2,1)}, bf16[9,128,1024]{2,1,0:T(8,128)(2,1)}, u32[]{:S(2)}, u32[]{:S(2)}) %collective-permute-start.1) | collective-permute-done | bytes 2359328 | tf_op jit(solution)/shard_map/ppermute | solution.py:14
  123.3 12.3 %all-to-all-done.1 = bf16[8,2,65536]{2,1,0:T(2,128)(2,1)} async-done(((bf16[8,2,65536]{2,1,0:T(2,128)(2,1)}), bf16[8,2,65536]{2,1,0:T(2,128)(2,1)}, u32[]{:S(2)}, u32[]{:S(2)}) %all-to-all-start.1) | async-done | bytes 2097184 | tf_op jit(solution)/shard_map/all_to_all | solution.py:101
  145.6 26.6 %collective-permute-done.2 = bf16[9,128,1024]{2,1,0:T(8,128)(2,1)} collective-permute-done((bf16[9,128,1024]{2,1,0:T(8,128)(2,1)}, bf16[9,128,1024]{2,1,0:T(8,128)(2,1)}, u32[]{:S(2)}, u32[]{:S(2)}) %collective-permute-start.2) | collective-permute-done | bytes 2359328 | tf_op jit(solution)/shard_map/ppermute | solution.py:14
  172.1 3.3 %constant_dynamic-update-slice_fusion.7 = bf16[9,1024,1024]{2,1,0:T(8,128)(2,1)} fusion(bf16[9,128,1024]{2,1,0:T(8,128)(2,1)} %collective-permute-done.2), kind=kLoop, calls=%fused_computation.96 | loop fusion | bytes 4718592
  175.4 3.3 %constant_dynamic-update-slice_fusion.6 = bf16[9,1024,1024]{2,1,0:T(8,128)(2,1)} fusion(bf16[9,1024,1024]{2,1,0:T(8,128)(2,1)} %constant_dynamic-update-slice_fusion.7, bf16[9,128,1024]{2,1,0:T(8,128)(2,1)} %collective-permute-done.1), kind=kLoop, calls=%fused_computation.95 | loop fusion | bytes 4718592
  178.7 3.3 %constant_dynamic-update-slice_fusion.5 = bf16[9,1024,1024]{2,1,0:T(8,128)(2,1)} fusion(bf16[9,1024,1024]{2,1,0:T(8,128)(2,1)} %constant_dynamic-update-slice_fusion.6, bf16[9,128,1024]{2,1,0:T(8,128)(2,1)} %collective-permute-done), kind=kLoop, calls=%fused_computation.94 | loop fusion | bytes 4718592
  183.6 3.2 %constant_dynamic-update-slice_fusion.3 = bf16[9,1024,1024]{2,1,0:T(8,128)(2,1)} fusion(bf16[9,1024,1024]{2,1,0:T(8,128)(2,1)} %constant_dynamic-update-slice_fusion.4, bf16[9,128,1024]{2,1,0:T(8,128)(2,1)} %collective-permute-done.2), kind=kLoop, calls=%fused_computation.92 | loop fusion | bytes 4718592
  186.9 3.2 %constant_dynamic-update-slice_fusion.2 = bf16[9,1024,1024]{2,1,0:T(8,128)(2,1)} fusion(bf16[9,1024,1024]{2,1,0:T(8,128)(2,1)} %constant_dynamic-update-slice_fusion.3, bf16[9,128,1024]{2,1,0:T(8,128)(2,1)} %collective-permute-done.1), kind=kLoop, calls=%fused_computation.91 | loop fusion | bytes 4718592
  190.1 3.3 %constant_dynamic-update-slice_fusion.1 = bf16[9,1024,1024]{2,1,0:T(8,128)(2,1)} fusion(bf16[9,1024,1024]{2,1,0:T(8,128)(2,1)} %constant_dynamic-update-slice_fusion.2, bf16[9,128,1024]{2,1,0:T(8,128)(2,1)} %collective-permute-done), kind=kLoop, calls=%fused_computation.90 | loop fusion | bytes 4718592
  195.1 8.5 %constant_dynamic-slice_fusion.1 = bf16[9,512,1024]{2,1,0:T(8,128)(2,1)} fusion(bf16[9,1024,1024]{2,1,0:T(8,128)(2,1)} %constant_dynamic-update-slice_fusion, s32[]{:T(128)S(6)} %select_n.14), kind=kLoop, calls=%fused_computation.123 | loop fusion | bytes 18874372 | tf_op jit(solution)/shard_map/jit(_roll_dynamic)/dynamic_slice | solution.py:17
  203.6 96.9 %while.11 = (s32[]{:T(128)}, f32[512,1024]{1,0:T(8,128)}, bf16[9,21]{1,0:T(8,128)(2,1)S(1)}, bf16[9,512,1024]{2,1,0:T(8,128)(2,1)}, s32[3]{0:T(128)S(1)}, /*index=5*/s32[]{:T(128)}, s32[]{:T(128)}) while((s32[]{:T(128)}, f32[512,1024]{1,0:T(8,128)}, bf16[9,21]{1,0:T(8,128)(2,1)S(1)}, bf16[9,512,1024]{2,1,0:T(8,128)(2,1)}, ...), condition=%wide.region_2.3_spmd.clone, body=%wide.region_1.2_spmd.clone.sunk | while | flops 422297600 | bytes 33489512 | solution.py:147
  204.2 4.0 %fusion.117 = bf16[1,3,128,128]{3,0,2,1:T(2,128)(2,1)S(1)} fusion(f32[3,21,128,128]{3,2,1,0:T(8,128)S(1)} %fusion.116, bf16[9,21]{1,0:T(8,128)(2,1)S(1)} %get-tuple-element.132, s32[]{:T(128)} %get-tuple-element.123), kind=kOutput, calls=%fused_computation.1.clone.1 | convolution fusion | flops 12386304 | bytes 4227588 | tf_op jit(solution)/shard_map/while/body/eval_jaxpr/cl,dlij->cdij/dot_general | solution.py:30
  213.5 4.0 %fusion.117 = bf16[1,3,128,128]{3,0,2,1:T(2,128)(2,1)S(1)} fusion(f32[3,21,128,128]{3,2,1,0:T(8,128)S(1)} %fusion.116, bf16[9,21]{1,0:T(8,128)(2,1)S(1)} %get-tuple-element.132, s32[]{:T(128)} %get-tuple-element.123), kind=kOutput, calls=%fused_computation.1.clone.1 | convolution fusion | flops 12386304 | bytes 4227588 | tf_op jit(solution)/shard_map/while/body/eval_jaxpr/cl,dlij->cdij/dot_general | solution.py:30
  220.4 3.5 %bitcast_add_fusion.4 = f32[512,1024]{1,0:T(8,128)} fusion(f32[128,4,1024]{2,0,1:T(8,128)S(1)} %add_add_fusion.2, f32[512,1024]{1,0:T(8,128)} %get-tuple-element.124, pred[]{:T(512)S(6)} %compare.12), kind=kLoop, calls=%fused_computation.5.clone.1 | loop fusion | flops 1048576 | bytes 6291457 | tf_op jit(solution)/shard_map/while/body/eval_jaxpr/add | solution.py:145
  224.5 4.0 %fusion.117 = bf16[1,3,128,128]{3,0,2,1:T(2,128)(2,1)S(1)} fusion(f32[3,21,128,128]{3,2,1,0:T(8,128)S(1)} %fusion.116, bf16[9,21]{1,0:T(8,128)(2,1)S(1)} %get-tuple-element.132, s32[]{:T(128)} %get-tuple-element.123), kind=kOutput, calls=%fused_computation.1.clone.1 | convolution fusion | flops 12386304 | bytes 4227588 | tf_op jit(solution)/shard_map/while/body/eval_jaxpr/cl,dlij->cdij/dot_general | solution.py:30
  231.3 3.5 %bitcast_add_fusion.4 = f32[512,1024]{1,0:T(8,128)} fusion(f32[128,4,1024]{2,0,1:T(8,128)S(1)} %add_add_fusion.2, f32[512,1024]{1,0:T(8,128)} %get-tuple-element.124, pred[]{:T(512)S(6)} %compare.12), kind=kLoop, calls=%fused_computation.5.clone.1 | loop fusion | flops 1048576 | bytes 6291457 | tf_op jit(solution)/shard_map/while/body/eval_jaxpr/add | solution.py:145
  235.4 4.0 %fusion.117 = bf16[1,3,128,128]{3,0,2,1:T(2,128)(2,1)S(1)} fusion(f32[3,21,128,128]{3,2,1,0:T(8,128)S(1)} %fusion.116, bf16[9,21]{1,0:T(8,128)(2,1)S(1)} %get-tuple-element.132, s32[]{:T(128)} %get-tuple-element.123), kind=kOutput, calls=%fused_computation.1.clone.1 | convolution fusion | flops 12386304 | bytes 4227588 | tf_op jit(solution)/shard_map/while/body/eval_jaxpr/cl,dlij->cdij/dot_general | solution.py:30
  242.3 3.5 %bitcast_add_fusion.4 = f32[512,1024]{1,0:T(8,128)} fusion(f32[128,4,1024]{2,0,1:T(8,128)S(1)} %add_add_fusion.2, f32[512,1024]{1,0:T(8,128)} %get-tuple-element.124, pred[]{:T(512)S(6)} %compare.12), kind=kLoop, calls=%fused_computation.5.clone.1 | loop fusion | flops 1048576 | bytes 6291457 | tf_op jit(solution)/shard_map/while/body/eval_jaxpr/add | solution.py:145
  246.4 4.0 %fusion.117 = bf16[1,3,128,128]{3,0,2,1:T(2,128)(2,1)S(1)} fusion(f32[3,21,128,128]{3,2,1,0:T(8,128)S(1)} %fusion.116, bf16[9,21]{1,0:T(8,128)(2,1)S(1)} %get-tuple-element.132, s32[]{:T(128)} %get-tuple-element.123), kind=kOutput, calls=%fused_computation.1.clone.1 | convolution fusion | flops 12386304 | bytes 4227588 | tf_op jit(solution)/shard_map/while/body/eval_jaxpr/cl,dlij->cdij/dot_general | solution.py:30
  253.2 3.5 %bitcast_add_fusion.4 = f32[512,1024]{1,0:T(8,128)} fusion(f32[128,4,1024]{2,0,1:T(8,128)S(1)} %add_add_fusion.2, f32[512,1024]{1,0:T(8,128)} %get-tuple-element.124, pred[]{:T(512)S(6)} %compare.12), kind=kLoop, calls=%fused_computation.5.clone.1 | loop fusion | flops 1048576 | bytes 6291457 | tf_op jit(solution)/shard_map/while/body/eval_jaxpr/add | solution.py:145
  257.3 4.0 %fusion.117 = bf16[1,3,128,128]{3,0,2,1:T(2,128)(2,1)S(1)} fusion(f32[3,21,128,128]{3,2,1,0:T(8,128)S(1)} %fusion.116, bf16[9,21]{1,0:T(8,128)(2,1)S(1)} %get-tuple-element.132, s32[]{:T(128)} %get-tuple-element.123), kind=kOutput, calls=%fused_computation.1.clone.1 | convolution fusion | flops 12386304 | bytes 4227588 | tf_op jit(solution)/shard_map/while/body/eval_jaxpr/cl,dlij->cdij/dot_general | solution.py:30
  264.2 3.5 %bitcast_add_fusion.4 = f32[512,1024]{1,0:T(8,128)} fusion(f32[128,4,1024]{2,0,1:T(8,128)S(1)} %add_add_fusion.2, f32[512,1024]{1,0:T(8,128)} %get-tuple-element.124, pred[]{:T(512)S(6)} %compare.12), kind=kLoop, calls=%fused_computation.5.clone.1 | loop fusion | flops 1048576 | bytes 6291457 | tf_op jit(solution)/shard_map/while/body/eval_jaxpr/add | solution.py:145
  268.3 4.0 %fusion.117 = bf16[1,3,128,128]{3,0,2,1:T(2,128)(2,1)S(1)} fusion(f32[3,21,128,128]{3,2,1,0:T(8,128)S(1)} %fusion.116, bf16[9,21]{1,0:T(8,128)(2,1)S(1)} %get-tuple-element.132, s32[]{:T(128)} %get-tuple-element.123), kind=kOutput, calls=%fused_computation.1.clone.1 | convolution fusion | flops 12386304 | bytes 4227588 | tf_op jit(solution)/shard_map/while/body/eval_jaxpr/cl,dlij->cdij/dot_general | solution.py:30
  275.1 3.5 %bitcast_add_fusion.4 = f32[512,1024]{1,0:T(8,128)} fusion(f32[128,4,1024]{2,0,1:T(8,128)S(1)} %add_add_fusion.2, f32[512,1024]{1,0:T(8,128)} %get-tuple-element.124, pred[]{:T(512)S(6)} %compare.12), kind=kLoop, calls=%fused_computation.5.clone.1 | loop fusion | flops 1048576 | bytes 6291457 | tf_op jit(solution)/shard_map/while/body/eval_jaxpr/add | solution.py:145
  279.2 4.0 %fusion.117 = bf16[1,3,128,128]{3,0,2,1:T(2,128)(2,1)S(1)} fusion(f32[3,21,128,128]{3,2,1,0:T(8,128)S(1)} %fusion.116, bf16[9,21]{1,0:T(8,128)(2,1)S(1)} %get-tuple-element.132, s32[]{:T(128)} %get-tuple-element.123), kind=kOutput, calls=%fused_computation.1.clone.1 | convolution fusion | flops 12386304 | bytes 4227588 | tf_op jit(solution)/shard_map/while/body/eval_jaxpr/cl,dlij->cdij/dot_general | solution.py:30
  286.1 3.5 %bitcast_add_fusion.4 = f32[512,1024]{1,0:T(8,128)} fusion(f32[128,4,1024]{2,0,1:T(8,128)S(1)} %add_add_fusion.2, f32[512,1024]{1,0:T(8,128)} %get-tuple-element.124, pred[]{:T(512)S(6)} %compare.12), kind=kLoop, calls=%fused_computation.5.clone.1 | loop fusion | flops 1048576 | bytes 6291457 | tf_op jit(solution)/shard_map/while/body/eval_jaxpr/add | solution.py:145
  290.2 4.0 %fusion.117 = bf16[1,3,128,128]{3,0,2,1:T(2,128)(2,1)S(1)} fusion(f32[3,21,128,128]{3,2,1,0:T(8,128)S(1)} %fusion.116, bf16[9,21]{1,0:T(8,128)(2,1)S(1)} %get-tuple-element.132, s32[]{:T(128)} %get-tuple-element.123), kind=kOutput, calls=%fused_computation.1.clone.1 | convolution fusion | flops 12386304 | bytes 4227588 | tf_op jit(solution)/shard_map/while/body/eval_jaxpr/cl,dlij->cdij/dot_general | solution.py:30
  297.0 3.5 %bitcast_add_fusion.4 = f32[512,1024]{1,0:T(8,128)} fusion(f32[128,4,1024]{2,0,1:T(8,128)S(1)} %add_add_fusion.2, f32[512,1024]{1,0:T(8,128)} %get-tuple-element.124, pred[]{:T(512)S(6)} %compare.12), kind=kLoop, calls=%fused_computation.5.clone.1 | loop fusion | flops 1048576 | bytes 6291457 | tf_op jit(solution)/shard_map/while/body/eval_jaxpr/add | solution.py:145
  (149 shorter events, 90.1 us)
Async XLA Ops:
  0.0 0.7 copy-start
  2.1 1.0 copy-start.4
  7.5 5.9 %copy-start.7 = (s32[1,1,16,1]{2,3,1,0:T(1,128)S(1)}, s32[1,1,16,1]{2,3,1,0:T(1,128)}, u32[]{:S(2)}) copy-start(s32[1,1,16,1]{2,3,1,0:T(1,128)} %param.13) | copy-start | bytes 196
  7.5 59.7 %copy-start.8 = (s32[1,1,16]{2,1,0:T(1,128)S(1)}, s32[1,1,16]{2,1,0:T(1,128)}, u32[]{:S(2)}) copy-start(s32[1,1,16]{2,1,0:T(1,128)} %param.14) | copy-start | bytes 196
  10.4 55.3 %collective-permute-start = (bf16[9,128,1024]{2,1,0:T(8,128)(2,1)S(1)}, bf16[9,128,1024]{2,1,0:T(8,128)(2,1)}, u32[]{:S(2)}, u32[]{:S(2)}) collective-permute-start(bf16[9,128,1024]{2,1,0:T(8,128)(2,1)S(1)} %copy.86), channel_id=1, source_target_pairs={{0,1},{1,2},{2,3},{3,0},{4,5},{5,6},{6,7},{7,4},{8,9},{9,10},{10,1... | collective-permute-start | bytes 7077896 | tf_op jit(solution)/shard_map/ppermute | solution.py:14
  65.7 53.6 %collective-permute-start.1 = (bf16[9,128,1024]{2,1,0:T(8,128)(2,1)}, bf16[9,128,1024]{2,1,0:T(8,128)(2,1)}, u32[]{:S(2)}, u32[]{:S(2)}) collective-permute-start(bf16[9,128,1024]{2,1,0:T(8,128)(2,1)} %collective-permute-done), channel_id=1, source_target_pairs={{0,1},{1,2},{2,3},{3,0},{4,5},{5,6},{6,7},{7,4},{8,9},{9,10},{10,1... | collective-permute-start | bytes 7077896 | tf_op jit(solution)/shard_map/ppermute | solution.py:14
  68.0 13.2 %all-to-all-start = ((bf16[8,1,2]{2,1,0:T(2,128)(2,1)}), bf16[8,1,2]{2,1,0:T(2,128)(2,1)S(1)}, u32[]{:S(2)}, u32[]{:S(2)}) async-start(bf16[8,1,2]{2,1,0:T(2,128)(2,1)} %all_to_all.12), calls=%async_computation | async-start | bytes 8192 | tf_op jit(solution)/shard_map/all_to_all | solution.py:102
  81.2 38.2 %copy-start.9 = (bf16[1,2,25]{2,1,0:T(2,128)(2,1)S(1)}, bf16[1,2,25]{2,1,0:T(2,128)(2,1)}, u32[]{:S(2)}) copy-start(bf16[1,2,25]{2,1,0:T(2,128)(2,1)} %param.21) | copy-start | bytes 304
  81.2 54.4 %all-to-all-start.1 = ((bf16[8,2,65536]{2,1,0:T(2,128)(2,1)}), bf16[8,2,65536]{2,1,0:T(2,128)(2,1)}, u32[]{:S(2)}, u32[]{:S(2)}) async-start(bf16[8,2,65536]{2,1,0:T(2,128)(2,1)} %reshape.116), calls=%async_computation.1 | async-start | bytes 4194304 | tf_op jit(solution)/shard_map/all_to_all | solution.py:101
  119.3 52.8 %collective-permute-start.2 = (bf16[9,128,1024]{2,1,0:T(8,128)(2,1)}, bf16[9,128,1024]{2,1,0:T(8,128)(2,1)}, u32[]{:S(2)}, u32[]{:S(2)}) collective-permute-start(bf16[9,128,1024]{2,1,0:T(8,128)(2,1)} %collective-permute-done.1), channel_id=1, source_target_pairs={{0,1},{1,2},{2,3},{3,0},{4,5},{5,6},{6,7},{7,4},{8,9},{9,10},{10,1... | collective-permute-start | bytes 7077896 | tf_op jit(solution)/shard_map/ppermute | solution.py:14
  119.3 2.1 copy-start.5
  119.4 2.1 copy-start.6
  119.4 2.2 copy-start.10
  300.5 3.0 copy-start.2
  310.5 1.2 copy-start.3
  318.7 1.9 copy-start.1
